TPU v7x, 256 devices: a whole 4x4x8 slice. The times are simulated.
256 devices in a mesh: outer: 16 (over z_hi, x, core), inner: 16 (over z_lo, y).
Axes of the slice: x: 4, y: 4, z: 8 (z_hi: 2, z_lo: 4; z = z_hi * 4 + z_lo), core: 2. Of those that a mesh axis runs over, the one named last changes fastest.
Arguments:
- tokens: bfloat16 [65536, 2048], P(('outer', 'inner')), may hold values from -6 to 6
- w_qkv: bfloat16 [2048, 3072], P('inner'), may hold values from -2.8 to 2.8
- w_out: bfloat16 [1024, 2048], P(None, 'inner'), may hold values from -1.5 to 1.5
- neighbours: int32 [256, 5], P(('outer', 'inner')), may hold values from -1 to 255, as said below
- counts: int32 [256], replicated, may hold values from 1 to 256, as said below
Outputs:
- attended: bfloat16 [65536, 2048], P(('outer', 'inner'))
Inputs may be any that keep to these rules, and one draw needn't show every extreme that they name: `neighbours`: slot 0 of row b is b itself; slots 1 and 2 are the blocks b - 16 and b + 16 (the same inner index in the previous and next slab of outer), slots 3 and 4 the blocks b - 1 and b + 1 of the same slab; a slot holds -1 where its block lies outside the grid of blocks, and may hold -1 otherwise. `counts`: some block is full.
All inputs are finite; a program needn't handle non-finite values.
Results may differ from a plain program's by a relative error of at most 0.0093.
Values may be sent and summed in bfloat16 or wider, within the bound.
A program may use at most 64 MiB of HBM per device.

v0:
```python
import jax
import jax.numpy as jnp
from jax import lax
from jax.sharding import PartitionSpec as P

HD = 128


def padded(block, sides, width):
    for axis, dim in sides:
        count = lax.axis_size(axis)
        forward = [(i, i + 1) for i in range(count - 1)]
        backward = [(target, source) for source, target in forward]
        low = lax.ppermute(
            lax.slice_in_dim(block, block.shape[dim] - width, None, axis=dim), axis, forward
        )
        high = lax.ppermute(lax.slice_in_dim(block, 0, width, axis=dim), axis, backward)
        block = jnp.concatenate([low, block, high], axis=dim)
    return block


def normalize(values_in):
    values = values_in.astype(jnp.float32)
    center = values - jnp.mean(values, axis=-1, keepdims=True)
    spread = jnp.mean(center * center, axis=-1, keepdims=True)
    return (center * lax.rsqrt(spread + 1e-05)).astype(jnp.bfloat16)


def per_device(tokens, w_qkv, w_out, neighbours, counts):
    normed = normalize(tokens)
    rows_here = normed.shape[0]
    heads_all = w_out.shape[0]
    head_size = HD
    projected = jnp.dot(
        normed,
        lax.all_gather(w_qkv, "inner", axis=0, tiled=True),
        preferred_element_type=jnp.float32,
    ).astype(jnp.bfloat16)
    queries = projected[:, :heads_all]
    keys_values = projected[:, heads_all:]
    slab_halo = padded(keys_values[None], (("outer", 0),), 1)
    row_halo = padded(keys_values[None], (("inner", 0),), 1)
    candidates = (keys_values, slab_halo[0], slab_halo[2], row_halo[0], row_halo[2])
    listed = neighbours[0]
    clipped = jnp.maximum(listed, 0)
    block_ids = jnp.arange(counts.shape[0], dtype=jnp.int32)
    lengths = jnp.sum(jnp.where(clipped[:, None] == block_ids[None, :], counts[None, :], 0), axis=1)
    positions = jnp.arange(rows_here, dtype=jnp.int32)
    usable = (listed[:, None] >= 0) & (positions[None, :] < lengths[:, None])
    allowed = usable.reshape(-1)
    score_scale = float(head_size) ** (-0.5)
    outputs = []
    for head_index in range(heads_all // head_size):
        offset_q = head_index * head_size
        offset_v = heads_all + offset_q
        query_head = queries[:, offset_q : offset_q + head_size]
        scores = (
            jnp.concatenate(
                [
                    jnp.einsum(
                        "qd,kd->qk",
                        query_head,
                        source_kv[:, offset_q : offset_q + head_size],
                        preferred_element_type=jnp.float32,
                    )
                    for source_kv in candidates
                ],
                axis=1,
            )
            * score_scale
        )
        masked = jnp.where(allowed[None, :], scores, -jnp.inf)
        largest = jnp.max(masked, axis=1, keepdims=True)
        weights = jnp.exp(masked - largest)
        totals = jnp.sum(weights, axis=1, keepdims=True)
        rounded = weights.astype(jnp.bfloat16)
        context = jnp.zeros((rows_here, head_size), jnp.float32)
        for slot_no in range(len(candidates)):
            context = context + jnp.dot(
                rounded[:, slot_no * rows_here : (slot_no + 1) * rows_here],
                candidates[slot_no][:, offset_v : offset_v + head_size],
                preferred_element_type=jnp.float32,
            )
        outputs.append((context / totals).astype(jnp.bfloat16))
    context_all = jnp.concatenate(outputs, axis=1)
    return jnp.dot(
        context_all,
        lax.all_gather(w_out, "inner", axis=1, tiled=True),
        preferred_element_type=jnp.float32,
    ).astype(jnp.bfloat16)


def solution(mesh):
    placed = (
        P(("outer", "inner"), None),
        P("inner", None),
        P(None, "inner"),
        P(("outer", "inner"), None),
        P(),
    )
    return jax.shard_map(
        per_device,
        mesh=mesh,
        in_specs=placed,
        out_specs=P(("outer", "inner"), None),
        check_vma=False,
    )
```

profile of v0, /device:TPU:152, one launch (start us, length us, event | category | flops | bytes accessed | tf_op | source)
XLA Modules:
  0.0 284.8 jit_solution(12477237379816694622)
XLA Ops:
  6.5 0.7 all-gather.3.cloned.1.call-update
  7.3 0.7 all-gather.5.cloned.1.call-update
  8.0 0.7 maximum_bitcast_fusion
  8.7 0.7 compare_bitcast_fusion
  9.3 0.2 convert_reduce_fusion
  9.6 0.4 fusion.2
  10.3 139.8 %all-gather.3.cloned.1.call-done = bf16[2048,3072]{1,0:T(8,128)(2,1)} async-done(((bf16[128,3072]{1,0:T(8,128)(2,1)}), bf16[2048,3072]{1,0:T(8,128)(2,1)}) %all-gather.3.cloned.1.call-update) | async-done | bytes 12582928 | tf_op jit(solution)/shard_map/all_gather | solution.py:36
  150.1 8.2 %convolution_convert_fusion = bf16[256,3072]{1,0:T(8,128)(2,1)S(1)} fusion(bf16[2048,3072]{1,0:T(8,128)(2,1)} %all-gather.3.cloned.1.call-done, bf16[256,2048]{1,0:T(8,128)(2,1)S(1)} %copy-done, f32[256]{0:T(256)S(1)} %add_rsqrt_fusion, f32[256]{0:T(256)S(1)} %broadcast_multiply_fusion), kind=kOutput, calls=%fused_computation | convolution fusion | flops 3224109056 | bytes 15206400 | tf_op jit(solution)/shard_map/dot_general | solution.py:34
  158.5 1.9 collective-permute-start
  160.4 9.7 %collective-permute-start.1 = (bf16[1,256,2048]{2,1,0:T(8,128)(2,1)S(1)}, bf16[1,256,2048]{2,1,0:T(8,128)(2,1)S(1)}, u32[]{:S(2)}, u32[]{:S(2)}) collective-permute-start(bf16[1,256,2048]{2,1,0:T(8,128)(2,1)S(1)} %slice_bitcast_fusion), channel_id=1, source_target_pairs={{16,0},{32,16},{48,32},{64,48},{80,64},{96,80},{112,96},{128,112},... | collective-permute-start | bytes 3145736 | tf_op jit(solution)/shard_map/ppermute | solution.py:17
  170.1 5.2 %collective-permute-start.2 = (bf16[1,256,2048]{2,1,0:T(8,128)(2,1)S(1)}, bf16[1,256,2048]{2,1,0:T(8,128)(2,1)S(1)}, u32[]{:S(2)}, u32[]{:S(2)}) collective-permute-start(bf16[1,256,2048]{2,1,0:T(8,128)(2,1)S(1)} %slice_bitcast_fusion), channel_id=1, source_target_pairs={{0,1},{1,2},{2,3},{3,4},{4,5},{5,6},{6,7},{7,8},{8,9},{9,10},{10,1... | collective-permute-start | bytes 3145736 | tf_op jit(solution)/shard_map/ppermute | solution.py:14
  175.3 2.1 collective-permute-start.3
  178.8 20.7 %collective-permute-done = bf16[1,256,2048]{2,1,0:T(8,128)(2,1)S(1)} collective-permute-done((bf16[1,256,2048]{2,1,0:T(8,128)(2,1)S(1)}, bf16[1,256,2048]{2,1,0:T(8,128)(2,1)S(1)}, u32[]{:S(2)}, u32[]{:S(2)}) %collective-permute-start) | collective-permute-done | bytes 1048608 | tf_op jit(solution)/shard_map/ppermute | solution.py:14
  199.7 0.2 convolution_dynamic-update-slice_fusion.38
  199.9 6.6 %collective-permute-done.1 = bf16[1,256,2048]{2,1,0:T(8,128)(2,1)S(1)} collective-permute-done((bf16[1,256,2048]{2,1,0:T(8,128)(2,1)S(1)}, bf16[1,256,2048]{2,1,0:T(8,128)(2,1)S(1)}, u32[]{:S(2)}, u32[]{:S(2)}) %collective-permute-start.1) | collective-permute-done | bytes 1048608 | tf_op jit(solution)/shard_map/ppermute | solution.py:17
  206.7 0.2 convolution_dynamic-update-slice_fusion.37
  206.9 21.2 %collective-permute-done.2 = bf16[1,256,2048]{2,1,0:T(8,128)(2,1)S(1)} collective-permute-done((bf16[1,256,2048]{2,1,0:T(8,128)(2,1)S(1)}, bf16[1,256,2048]{2,1,0:T(8,128)(2,1)S(1)}, u32[]{:S(2)}, u32[]{:S(2)}) %collective-permute-start.2) | collective-permute-done | bytes 1048608 | tf_op jit(solution)/shard_map/ppermute | solution.py:14
  228.4 26.1 %collective-permute-done.3 = bf16[1,256,2048]{2,1,0:T(8,128)(2,1)S(1)} collective-permute-done((bf16[1,256,2048]{2,1,0:T(8,128)(2,1)S(1)}, bf16[1,256,2048]{2,1,0:T(8,128)(2,1)S(1)}, u32[]{:S(2)}, u32[]{:S(2)}) %collective-permute-start.3) | collective-permute-done | bytes 1048608 | tf_op jit(solution)/shard_map/ppermute | solution.py:17
  255.3 0.2 convolution_dynamic-update-slice_fusion.31
  255.7 0.2 convolution_dynamic-update-slice_fusion.28
  259.6 0.4 fusion.11
  259.9 2.0 fusion.69
  261.9 0.2 fusion.127
  262.1 0.2 fusion.129
  262.4 0.2 fusion.133
  262.6 2.3 fusion.67
  264.9 0.2 fusion.119
  265.1 0.2 fusion.121
  265.3 0.2 fusion.125
  265.6 0.2 fusion.111
  265.8 0.2 fusion.113
  266.0 0.2 fusion.117
  266.2 0.2 fusion.103
  266.5 0.2 fusion.105
  266.7 0.2 fusion.109
  266.9 0.2 fusion.95
  267.2 0.2 fusion.97
  267.4 0.2 fusion.101
  267.6 0.2 fusion.87
  267.9 0.2 fusion.89
  268.1 0.2 fusion.93
  268.3 0.2 fusion.79
  268.5 0.2 fusion.81
  268.8 0.2 fusion.85
  269.0 0.2 fusion.71
  269.2 0.2 fusion.73
  269.5 0.2 fusion.77
  269.7 0.2 convolution_add_fusion.15
  269.9 0.2 convolution_add_fusion.13
  270.2 0.2 convolution_add_fusion.11
  270.4 0.2 convolution_add_fusion.9
  270.6 0.2 convolution_add_fusion.7
  270.9 0.2 convolution_add_fusion.5
  271.1 0.2 convolution_add_fusion.3
  271.3 0.2 convolution_add_fusion.1
  271.5 0.2 fusion.51
  271.8 0.2 fusion.49
  272.0 0.2 fusion.47
  272.3 0.2 fusion.45
  272.5 0.2 fusion.43
  272.8 0.2 fusion.41
  273.1 0.2 fusion.39
  273.3 0.2 fusion.37
  273.6 4.4 %convolution_convert_fusion.1 = bf16[256,2048]{1,0:T(8,128)(2,1)} fusion(bf16[256,1024]{1,0:T(8,128)(2,1)S(1)} %fusion.37, bf16[1024,2048]{1,0:T(8,128)(2,1)} %all-gather.5.cloned.1.call-done), kind=kOutput, calls=%fused_computation.3 | convolution fusion | flops 1074266112 | bytes 5767168 | tf_op jit(solution)/shard_map/dot_general | solution.py:86
  (49 shorter events, 7.1 us)
Async XLA Ops:
  6.5 2.8 copy-start
  6.5 143.5 %all-gather.3.cloned.1.call-start = ((), (), s32[]{:S(2)}) async-start(), calls=%async_computation | async-start | bytes 13369344 | tf_op jit(solution)/shard_map/all_gather | solution.py:36
  7.3 2.7 copy-start.1
  7.3 266.3 %all-gather.5.cloned.1.call-start = ((), (), s32[]{:S(2)}) async-start(), calls=%async_computation.1 | async-start | bytes 4456448 | tf_op jit(solution)/shard_map/all_gather | solution.py:88
  158.5 41.0 %collective-permute-start = (bf16[1,256,2048]{2,1,0:T(8,128)(2,1)S(1)}, bf16[1,256,2048]{2,1,0:T(8,128)(2,1)S(1)}, u32[]{:S(2)}, u32[]{:S(2)}) collective-permute-start(bf16[1,256,2048]{2,1,0:T(8,128)(2,1)S(1)} %slice_bitcast_fusion), channel_id=1, source_target_pairs={{0,16},{16,32},{32,48},{48,64},{64,80},{80,96},{96,112},{112,128},... | collective-permute-start | bytes 3145736 | tf_op jit(solution)/shard_map/ppermute | solution.py:14
  160.4 46.0 %collective-permute-start.1 = (bf16[1,256,2048]{2,1,0:T(8,128)(2,1)S(1)}, bf16[1,256,2048]{2,1,0:T(8,128)(2,1)S(1)}, u32[]{:S(2)}, u32[]{:S(2)}) collective-permute-start(bf16[1,256,2048]{2,1,0:T(8,128)(2,1)S(1)} %slice_bitcast_fusion), channel_id=1, source_target_pairs={{16,0},{32,16},{48,32},{64,48},{80,64},{96,80},{112,96},{128,112},... | collective-permute-start | bytes 3145736 | tf_op jit(solution)/shard_map/ppermute | solution.py:17
  170.1 57.9 %collective-permute-start.2 = (bf16[1,256,2048]{2,1,0:T(8,128)(2,1)S(1)}, bf16[1,256,2048]{2,1,0:T(8,128)(2,1)S(1)}, u32[]{:S(2)}, u32[]{:S(2)}) collective-permute-start(bf16[1,256,2048]{2,1,0:T(8,128)(2,1)S(1)} %slice_bitcast_fusion), channel_id=1, source_target_pairs={{0,1},{1,2},{2,3},{3,4},{4,5},{5,6},{6,7},{7,8},{8,9},{9,10},{10,1... | collective-permute-start | bytes 3145736 | tf_op jit(solution)/shard_map/ppermute | solution.py:14
  175.3 79.2 %collective-permute-start.3 = (bf16[1,256,2048]{2,1,0:T(8,128)(2,1)S(1)}, bf16[1,256,2048]{2,1,0:T(8,128)(2,1)S(1)}, u32[]{:S(2)}, u32[]{:S(2)}) collective-permute-start(bf16[1,256,2048]{2,1,0:T(8,128)(2,1)S(1)} %slice_bitcast_fusion), channel_id=1, source_target_pairs={{1,0},{2,1},{3,2},{4,3},{5,4},{6,5},{7,6},{8,7},{9,8},{10,9},{11,1... | collective-permute-start | bytes 3145736 | tf_op jit(solution)/shard_map/ppermute | solution.py:17
Sparse Core Ops, SparseCore 0:
  9.1 140.9 all-gather.2
  151.8 107.4 all-gather.4
where the time goes:
time: 285 us
  waiting for transfers between devices  216 us (76%)
  matrix products  29 us (10%)
  starting transfers between devices  18.9 us (7%)
  between operations  14.1 us (5%)
  other arithmetic  6.84 us (2%)
    all_gather x1, waiting for transfers between devices, per_device(): lax.all_gather(w_qkv, 'inner', axis=0, tiled=True)  140 us
    ppermute x2, waiting for transfers between devices, padded(): lax.ppermute(lax.slice_in_dim(block, block.shape[dim] - width, None, axis...  41.9 us
    ppermute x2, waiting for transfers between devices, padded(): lax.ppermute(lax.slice_in_dim(block, 0, width, axis=dim), axis, backward)  32.8 us
    ppermute x2, starting transfers between devices, padded(): lax.ppermute(lax.slice_in_dim(block, 0, width, axis=dim), axis, backward)  11.8 us
    dot_general x40, matrix products, per_device(): jnp.dot(rounded[:, slot_no * rows_here:(slot_no + 1) * rows_here], candid...  9.07 us
    dot_general x1, matrix products, per_device(): jnp.dot(normed, lax.all_gather(w_qkv, 'inner', axis=0, tiled=True), prefe...  8.16 us
    dot_general x40, matrix products, per_device(): jnp.einsum('qd,kd->qk', query_head, source_kv[:, offset_q:offset_q + head...  7.37 us
    ppermute x2, starting transfers between devices, padded(): lax.ppermute(lax.slice_in_dim(block, block.shape[dim] - width, None, axis...  7.12 us
  transfers between devices with their start and end apart: 6, of which 5 were waited for; matrix products, arithmetic and copies ran while one was open for 11% of the time, Pallas kernels for 0%

commit v1 on v0

--- a/solution.py
+++ b/solution.py
@@ -4,6 +4,13 @@
 from jax.sharding import PartitionSpec as P
 
 HD = 128
+
+
+def gather_over(shard, axis, dim):
+    peers = lax.axis_size(axis)
+    blocks = jnp.stack([shard for _ in range(peers)])
+    blocks = lax.all_to_all(blocks, axis, split_axis=0, concat_axis=0)
+    return jnp.concatenate(blocks, axis=dim)
 
 
 def padded(block, sides, width):
@@ -32,9 +39,7 @@
     heads_all = w_out.shape[0]
     head_size = HD
     projected = jnp.dot(
-        normed,
-        lax.all_gather(w_qkv, "inner", axis=0, tiled=True),
-        preferred_element_type=jnp.float32,
+        normed, gather_over(w_qkv, "inner", 0), preferred_element_type=jnp.float32
     ).astype(jnp.bfloat16)
     queries = projected[:, :heads_all]
     keys_values = projected[:, heads_all:]

time: 285 us -> 436 us (1.53); the launches traced: 285 us -> 430 us
  waiting for transfers between devices: 216 us -> 322 us
  starting transfers between devices: 18.9 us -> 52.5 us
  local copies, waits for them, and re-layouts: 0.1 us -> 7.3 us
    all_to_all x0 -> x1, waiting for transfers between devices: none -> 293 us  [gather_over(): blocks = lax.all_to_all(blocks, axis, split_axis=0, concat_axis=0)]
    all_gather x1 -> x0, waiting for transfers between devices: 140 us -> none  [per_device(): lax.all_gather(w_qkv, 'inner', axis=0, tiled=True)]
    ppermute x2, waiting for transfers between devices: 41.9 us -> 11.1 us  [padded(): lax.ppermute(lax.slice_in_dim(block, block.shape[dim] - width, None, axis...]
    ppermute x2, starting transfers between devices: 7.12 us -> 34.5 us  [padded(): lax.ppermute(lax.slice_in_dim(block, block.shape[dim] - width, None, axis...]
    ppermute x2, waiting for transfers between devices: 32.8 us -> 17.1 us  [padded(): lax.ppermute(lax.slice_in_dim(block, 0, width, axis=dim), axis, backward)]
    another operation x0 -> x1, local copies, waits for them, and re-layouts: none -> 7.2 us  [gather_over(): blocks = jnp.stack([shard for _ in range(peers)])]
    all_to_all x0 -> x1, starting transfers between devices: none -> 6.2 us  [gather_over(): blocks = lax.all_to_all(blocks, axis, split_axis=0, concat_axis=0)]
  transfers between devices with their start and end apart: 6 -> 6, of which waited for: 5 -> 3; matrix products, arithmetic and copies ran while one was open for 11% -> 7% of each run, Pallas kernels for 0% -> 0%
where the time goes in v1:
time: 436 us; the launch traced here: 430 us
  waiting for transfers between devices  322 us (74%)
  starting transfers between devices  52.5 us (12%)
  matrix products  29 us (7%)
  between operations  14.1 us (3%)
  local copies, waits for them, and re-layouts  7.3 us (2%)
  other arithmetic  5.53 us (1%)
    all_to_all x1, waiting for transfers between devices, gather_over(): blocks = lax.all_to_all(blocks, axis, split_axis=0, concat_axis=0)  293 us
    ppermute x2, starting transfers between devices, padded(): lax.ppermute(lax.slice_in_dim(block, block.shape[dim] - width, None, axis...  34.5 us
    ppermute x2, waiting for transfers between devices, padded(): lax.ppermute(lax.slice_in_dim(block, 0, width, axis=dim), axis, backward)  17.1 us
    ppermute x2, starting transfers between devices, padded(): lax.ppermute(lax.slice_in_dim(block, 0, width, axis=dim), axis, backward)  11.8 us
    ppermute x2, waiting for transfers between devices, padded(): lax.ppermute(lax.slice_in_dim(block, block.shape[dim] - width, None, axis...  11.1 us
    dot_general x40, matrix products, per_device(): jnp.dot(rounded[:, slot_no * rows_here:(slot_no + 1) * rows_here], candid...  9.07 us
  transfers between devices with their start and end apart: 6, of which 3 were waited for; matrix products, arithmetic and copies ran while one was open for 7% of the time, Pallas kernels for 0%

profile of v1, /device:TPU:152, one launch (start us, length us, event | category | flops | bytes accessed | tf_op | source)
XLA Modules:
  0.0 430.2 jit_solution(13716540347844866143)
XLA Ops:
  6.5 7.2 %stack.2 = bf16[16,128,3072]{2,1,0:T(8,128)(2,1)} broadcast(bf16[128,3072]{1,0:T(8,128)(2,1)} %param.6), dimensions={1,2} | broadcast | bytes 13369344 | tf_op jit(solution)/shard_map/stack | solution.py:11
  13.7 6.2 %all-to-all-start = ((bf16[16,128,3072]{2,1,0:T(8,128)(2,1)}), bf16[16,128,3072]{2,1,0:T(8,128)(2,1)}, u32[]{:S(2)}, u32[]{:S(2)}) async-start(bf16[16,128,3072]{2,1,0:T(8,128)(2,1)} %stack.2), calls=%async_computation | async-start | bytes 25165824 | tf_op jit(solution)/shard_map/all_to_all | solution.py:12
  20.0 0.7 all-gather.2.cloned.1.call-update
  21.0 0.2 convert_reduce_fusion
  21.2 0.4 fusion.2
  21.7 292.9 %all-to-all-done = bf16[16,128,3072]{2,1,0:T(8,128)(2,1)} async-done(((bf16[16,128,3072]{2,1,0:T(8,128)(2,1)}), bf16[16,128,3072]{2,1,0:T(8,128)(2,1)}, u32[]{:S(2)}, u32[]{:S(2)}) %all-to-all-start) | async-done | bytes 12582944 | tf_op jit(solution)/shard_map/all_to_all | solution.py:12
  314.5 8.2 %convolution_convert_fusion = bf16[256,3072]{1,0:T(8,128)(2,1)S(1)} fusion(bf16[2048,3072]{1,0:T(8,128)(2,1)} %bitcast.2, bf16[256,2048]{1,0:T(8,128)(2,1)S(1)} %copy-done, f32[256]{0:T(256)S(1)} %add_rsqrt_fusion, f32[256]{0:T(256)S(1)} %broadcast_multiply_fusion), kind=kOutput, calls=%fused_computation | convolution fusion | flops 3224109056 | bytes 15206400 | tf_op jit(solution)/shard_map/dot_general | solution.py:41
  323.0 1.9 collective-permute-start
  324.9 9.7 %collective-permute-start.1 = (bf16[1,256,2048]{2,1,0:T(8,128)(2,1)S(1)}, bf16[1,256,2048]{2,1,0:T(8,128)(2,1)S(1)}, u32[]{:S(2)}, u32[]{:S(2)}) collective-permute-start(bf16[1,256,2048]{2,1,0:T(8,128)(2,1)S(1)} %slice_bitcast_fusion), channel_id=1, source_target_pairs={{16,0},{32,16},{48,32},{64,48},{80,64},{96,80},{112,96},{128,112},... | collective-permute-start | bytes 3145736 | tf_op jit(solution)/shard_map/ppermute | solution.py:24
  334.6 32.6 %collective-permute-start.2 = (bf16[1,256,2048]{2,1,0:T(8,128)(2,1)S(1)}, bf16[1,256,2048]{2,1,0:T(8,128)(2,1)S(1)}, u32[]{:S(2)}, u32[]{:S(2)}) collective-permute-start(bf16[1,256,2048]{2,1,0:T(8,128)(2,1)S(1)} %slice_bitcast_fusion), channel_id=1, source_target_pairs={{0,1},{1,2},{2,3},{3,4},{4,5},{5,6},{6,7},{7,8},{8,9},{9,10},{10,1... | collective-permute-start | bytes 3145736 | tf_op jit(solution)/shard_map/ppermute | solution.py:21
  367.2 2.1 collective-permute-start.3
  369.5 0.2 convolution_dynamic-update-slice_fusion.34
  370.0 0.2 convolution_dynamic-update-slice_fusion.19
  370.2 0.2 convolution_dynamic-update-slice_fusion.14
  370.4 0.2 convolution_dynamic-update-slice_fusion.9
  370.8 0.2 convolution_dynamic-update-slice_fusion.38
  371.2 0.2 convolution_dynamic-update-slice_fusion.37
  371.4 11.1 %collective-permute-done.2 = bf16[1,256,2048]{2,1,0:T(8,128)(2,1)S(1)} collective-permute-done((bf16[1,256,2048]{2,1,0:T(8,128)(2,1)S(1)}, bf16[1,256,2048]{2,1,0:T(8,128)(2,1)S(1)}, u32[]{:S(2)}, u32[]{:S(2)}) %collective-permute-start.2) | collective-permute-done | bytes 1048608 | tf_op jit(solution)/shard_map/ppermute | solution.py:21
  382.9 17.1 %collective-permute-done.3 = bf16[1,256,2048]{2,1,0:T(8,128)(2,1)S(1)} collective-permute-done((bf16[1,256,2048]{2,1,0:T(8,128)(2,1)S(1)}, bf16[1,256,2048]{2,1,0:T(8,128)(2,1)S(1)}, u32[]{:S(2)}, u32[]{:S(2)}) %collective-permute-start.3) | collective-permute-done | bytes 1048608 | tf_op jit(solution)/shard_map/ppermute | solution.py:24
  400.1 0.2 convolution_dynamic-update-slice_fusion.35
  404.9 0.4 fusion.11
  405.3 2.0 fusion.69
  407.3 0.2 fusion.127
  407.5 0.2 fusion.129
  407.7 0.2 fusion.133
  408.0 2.3 fusion.67
  410.3 0.2 fusion.119
  410.5 0.2 fusion.121
  410.7 0.2 fusion.125
  410.9 0.2 fusion.111
  411.2 0.2 fusion.113
  411.4 0.2 fusion.117
  411.6 0.2 fusion.103
  411.9 0.2 fusion.105
  412.1 0.2 fusion.109
  412.3 0.2 fusion.95
  412.6 0.2 fusion.97
  412.8 0.2 fusion.101
  413.0 0.2 fusion.87
  413.2 0.2 fusion.89
  413.5 0.2 fusion.93
  413.7 0.2 fusion.79
  413.9 0.2 fusion.81
  414.2 0.2 fusion.85
  414.4 0.2 fusion.71
  414.6 0.2 fusion.73
  414.8 0.2 fusion.77
  415.1 0.2 convolution_add_fusion.15
  415.3 0.2 convolution_add_fusion.13
  415.5 0.2 convolution_add_fusion.11
  415.8 0.2 convolution_add_fusion.9
  416.0 0.2 convolution_add_fusion.7
  416.2 0.2 convolution_add_fusion.5
  416.5 0.2 convolution_add_fusion.3
  416.7 0.2 convolution_add_fusion.1
  416.9 0.2 fusion.51
  417.2 0.2 fusion.49
  417.4 0.2 fusion.47
  417.7 0.2 fusion.45
  417.9 0.2 fusion.43
  418.2 0.2 fusion.41
  418.4 0.2 fusion.39
  418.7 0.2 fusion.37
  419.0 4.4 %convolution_convert_fusion.1 = bf16[256,2048]{1,0:T(8,128)(2,1)} fusion(bf16[256,1024]{1,0:T(8,128)(2,1)S(1)} %fusion.37, bf16[1024,2048]{1,0:T(8,128)(2,1)} %all-gather.2.cloned.1.call-done), kind=kOutput, calls=%fused_computation.3 | convolution fusion | flops 1074266112 | bytes 5767168 | tf_op jit(solution)/shard_map/dot_general | solution.py:91
  (51 shorter events, 6.5 us)
Async XLA Ops:
  13.7 6.9 %copy-start.2 = (s32[1,5]{1,0:T(1,128)S(1)}, s32[1,5]{1,0:T(1,128)}, u32[]{:S(2)}) copy-start(s32[1,5]{1,0:T(1,128)} %param.8) | copy-start | bytes 64
  13.7 7.0 %copy-start.1 = (s32[256]{0:T(256)S(1)}, s32[256]{0:T(256)}, u32[]{:S(2)}) copy-start(s32[256]{0:T(256)} %param.9) | copy-start | bytes 3076
  13.7 7.3 %copy-start = (bf16[256,2048]{1,0:T(8,128)(2,1)S(1)}, bf16[256,2048]{1,0:T(8,128)(2,1)}, u32[]{:S(2)}) copy-start(bf16[256,2048]{1,0:T(8,128)(2,1)} %param.5) | copy-start | bytes 3145732
  13.7 300.8 %all-to-all-start = ((bf16[16,128,3072]{2,1,0:T(8,128)(2,1)}), bf16[16,128,3072]{2,1,0:T(8,128)(2,1)}, u32[]{:S(2)}, u32[]{:S(2)}) async-start(bf16[16,128,3072]{2,1,0:T(8,128)(2,1)} %stack.2), calls=%async_computation | async-start | bytes 25165824 | tf_op jit(solution)/shard_map/all_to_all | solution.py:12
  19.9 399.0 %all-gather.2.cloned.1.call-start = ((), (), s32[]{:S(2)}) async-start(), calls=%async_computation.1 | async-start | bytes 4456448 | tf_op jit(solution)/shard_map/all_gather | solution.py:93
  323.0 47.7 %collective-permute-start = (bf16[1,256,2048]{2,1,0:T(8,128)(2,1)S(1)}, bf16[1,256,2048]{2,1,0:T(8,128)(2,1)S(1)}, u32[]{:S(2)}, u32[]{:S(2)}) collective-permute-start(bf16[1,256,2048]{2,1,0:T(8,128)(2,1)S(1)} %slice_bitcast_fusion), channel_id=1, source_target_pairs={{0,16},{16,32},{32,48},{48,64},{64,80},{80,96},{96,112},{112,128},... | collective-permute-start | bytes 3145736 | tf_op jit(solution)/shard_map/ppermute | solution.py:21
  324.9 46.1 %collective-permute-start.1 = (bf16[1,256,2048]{2,1,0:T(8,128)(2,1)S(1)}, bf16[1,256,2048]{2,1,0:T(8,128)(2,1)S(1)}, u32[]{:S(2)}, u32[]{:S(2)}) collective-permute-start(bf16[1,256,2048]{2,1,0:T(8,128)(2,1)S(1)} %slice_bitcast_fusion), channel_id=1, source_target_pairs={{16,0},{32,16},{48,32},{64,48},{80,64},{96,80},{112,96},{128,112},... | collective-permute-start | bytes 3145736 | tf_op jit(solution)/shard_map/ppermute | solution.py:24
  334.6 47.9 %collective-permute-start.2 = (bf16[1,256,2048]{2,1,0:T(8,128)(2,1)S(1)}, bf16[1,256,2048]{2,1,0:T(8,128)(2,1)S(1)}, u32[]{:S(2)}, u32[]{:S(2)}) collective-permute-start(bf16[1,256,2048]{2,1,0:T(8,128)(2,1)S(1)} %slice_bitcast_fusion), channel_id=1, source_target_pairs={{0,1},{1,2},{2,3},{3,4},{4,5},{5,6},{6,7},{7,8},{8,9},{9,10},{10,1... | collective-permute-start | bytes 3145736 | tf_op jit(solution)/shard_map/ppermute | solution.py:21
  367.2 32.8 %collective-permute-start.3 = (bf16[1,256,2048]{2,1,0:T(8,128)(2,1)S(1)}, bf16[1,256,2048]{2,1,0:T(8,128)(2,1)S(1)}, u32[]{:S(2)}, u32[]{:S(2)}) collective-permute-start(bf16[1,256,2048]{2,1,0:T(8,128)(2,1)S(1)} %slice_bitcast_fusion), channel_id=1, source_target_pairs={{1,0},{2,1},{3,2},{4,3},{5,4},{6,5},{7,6},{8,7},{9,8},{10,9},{11,1... | collective-permute-start | bytes 3145736 | tf_op jit(solution)/shard_map/ppermute | solution.py:24
Sparse Core Ops, SparseCore 0:
  22.5 294.2 all-gather.1
